TPU v7x, 32 devices: a whole 2x2x4 slice. The times are simulated.
32 devices in a mesh: rep: 4 (over y, x), shard: 8 (over z, core).
Axes of the slice: x: 2, y: 2, z: 4, core: 2. Of those that a mesh axis runs over, the one named last changes fastest.
Arguments:
- latents_in: float32 [32, 256, 768], P(('rep', 'shard')), may hold values from -6 to 6
- conditioning: float32 [32, 768], P(('rep', 'shard')), may hold values from -6 to 6
- cotangent: float32 [32, 256, 768], P(('rep', 'shard')), may hold values from -6 to 6
- ada_weight: bfloat16 [768, 4608], P(None, 'shard'), may hold values from -0.21875 to 0.21875
- ada_bias: bfloat16 [4608], P('shard'), may hold values from -3 to 3
- qkv_weight: bfloat16 [768, 2304], P(None, 'shard'), may hold values from -0.21875 to 0.21875
- query_bias: bfloat16 [768], P('shard'), may hold values from -6 to 6
- value_bias: bfloat16 [768], P('shard'), may hold values from -6 to 6
- proj_weight: bfloat16 [768, 768], P(None, 'shard'), may hold values from -1.75 to 1.75
- proj_bias: bfloat16 [768], P('shard'), may hold values from -6 to 6
- fc1_weight: bfloat16 [768, 3072], P(None, 'shard'), may hold values from -0.21875 to 0.21875
- fc1_bias: bfloat16 [3072], P('shard'), may hold values from -6 to 6
- fc2_weight: bfloat16 [3072, 768], P(None, 'shard'), may hold values from -0.109375 to 0.109375
- fc2_bias: bfloat16 [768], P('shard'), may hold values from -6 to 6
Outputs:
- block_out: float32 [32, 256, 768], P(('rep', 'shard'))
- grad_input: float32 [32, 256, 768], P(('rep', 'shard'))
- grad_cond: float32 [32, 768], P(('rep', 'shard'))
- grad_ada_weight: float32 [768, 4608], P(None, 'shard')
- grad_ada_bias: float32 [4608], P('shard')
- grad_qkv_weight: float32 [768, 2304], P(None, 'shard')
- grad_query_bias: float32 [768], P('shard')
- grad_value_bias: float32 [768], P('shard')
- grad_proj_weight: float32 [768, 768], P(None, 'shard')
- grad_proj_bias: float32 [768], P('shard')
- grad_fc1_weight: float32 [768, 3072], P(None, 'shard')
- grad_fc1_bias: float32 [3072], P('shard')
- grad_fc2_weight: float32 [3072, 768], P(None, 'shard')
- grad_fc2_bias: float32 [768], P('shard')
All inputs are finite; a program needn't handle non-finite values.
Results may differ from a plain program's by a relative error of at most 0.01.
The roundings to bfloat16 on the way count: a program that leaves them out, or rounds other values in their place, can miss the bound.
Values may be sent and summed in bfloat16 or wider, within the bound.
No kernel may reach another device: no remote copies, remote signals or barrier semaphores. Data moves between devices by JAX's collectives and lax.ppermute only.
A program may use at most 192 MiB of HBM per device.

v0:
```python
import math
import jax
import jax.numpy as jnp
from jax import lax
from jax.sharding import PartitionSpec as P

HEAD = 64
gelu_scale = math.sqrt(2.0 / math.pi)
gelu_cubic = 0.044715
norm_eps = 1e-06


def layer_norm(values):
    center = values - jnp.mean(values, axis=-1, keepdims=True)
    variance = jnp.mean(center * center, axis=-1, keepdims=True)
    inv_std = lax.rsqrt(variance + norm_eps)
    return (center * inv_std, inv_std)


def norm_back(grad_normed, normed, inv_std):
    return inv_std * (
        grad_normed
        - jnp.mean(grad_normed, axis=-1, keepdims=True)
        - normed * jnp.mean(grad_normed * normed, axis=-1, keepdims=True)
    )


def head_product(form, left, right):
    return jnp.einsum(form, left, right, preferred_element_type=jnp.float32)


def flat_rows(values):
    return values.reshape(-1, values.shape[-1])


def matmul(left, right):
    return jnp.dot(left, right, preferred_element_type=jnp.float32)


def forward_all(latents, conds, weights):
    (
        ada_weight,
        ada_bias,
        qkv_weight,
        query_bias,
        value_bias,
        proj_weight,
        proj_bias,
        fc1_weight,
        fc1_bias,
        fc2_weight,
        fc2_bias,
    ) = weights
    count, seq_len, width = latents.shape
    head_count = width // HEAD
    sigmoid_c = jax.nn.sigmoid(conds)
    cond_act = (conds * sigmoid_c).astype(jnp.bfloat16)
    modulation = matmul(cond_act, ada_weight) + ada_bias.astype(jnp.float32)
    mods = [piece[:, None, :] for piece in jnp.split(modulation, 6, axis=1)]
    shift_one, scale_one, gate_one, shift_two, scale_two, gate_two = mods
    normed_one, inv_one = layer_norm(latents)
    hidden_one = (normed_one * (1.0 + scale_one) + shift_one).astype(jnp.bfloat16)
    qkv_rows = matmul(flat_rows(hidden_one), qkv_weight)
    head_shape = (count, seq_len, head_count, HEAD)
    query_heads = (
        (qkv_rows[:, :width] + query_bias.astype(jnp.float32))
        .astype(jnp.bfloat16)
        .reshape(head_shape)
    )
    key_heads = qkv_rows[:, width : 2 * width].astype(jnp.bfloat16).reshape(head_shape)
    value_heads = (
        (qkv_rows[:, 2 * width :] + value_bias.astype(jnp.float32))
        .astype(jnp.bfloat16)
        .reshape(head_shape)
    )
    scores = head_product("lqhd,lkhd->lhqk", query_heads, key_heads) * HEAD ** (-0.5)
    row_max = jnp.max(scores, axis=-1, keepdims=True)
    log_total = row_max + jnp.log(jnp.sum(jnp.exp(scores - row_max), axis=-1, keepdims=True))
    prob_low = jnp.exp(scores - log_total).astype(jnp.bfloat16)
    attended = (
        head_product("lhqk,lkhd->lqhd", prob_low, value_heads)
        .reshape(count, seq_len, width)
        .astype(jnp.bfloat16)
    )
    attn_out = (matmul(flat_rows(attended), proj_weight) + proj_bias.astype(jnp.float32)).reshape(
        count, seq_len, width
    )
    resid_mid = latents + gate_one * attn_out
    normed_two, inv_two = layer_norm(resid_mid)
    hidden_two = (normed_two * (1.0 + scale_two) + shift_two).astype(jnp.bfloat16)
    fc1_pre = (matmul(flat_rows(hidden_two), fc1_weight) + fc1_bias.astype(jnp.float32)).reshape(
        count, seq_len, -1
    )
    tanh_inner = jnp.tanh(gelu_scale * (fc1_pre + gelu_cubic * fc1_pre * fc1_pre * fc1_pre))
    fc1_act = (0.5 * fc1_pre * (1.0 + tanh_inner)).astype(jnp.bfloat16)
    mlp_out = (matmul(flat_rows(fc1_act), fc2_weight) + fc2_bias.astype(jnp.float32)).reshape(
        count, seq_len, width
    )
    block_out = resid_mid + gate_two * mlp_out
    saved = (
        conds,
        sigmoid_c,
        cond_act,
        modulation,
        normed_one,
        inv_one,
        hidden_one,
        query_heads,
        key_heads,
        value_heads,
        log_total,
        attended,
        attn_out,
        normed_two,
        inv_two,
        hidden_two,
        fc1_pre,
        tanh_inner,
        fc1_act,
        mlp_out,
    )
    return (block_out, saved)


def backward_all(cotangent, saved, weights, arrange):
    (
        ada_weight,
        ada_bias,
        qkv_weight,
        query_bias,
        value_bias,
        proj_weight,
        proj_bias,
        fc1_weight,
        fc1_bias,
        fc2_weight,
        fc2_bias,
    ) = weights
    (
        conds,
        sigmoid_c,
        cond_act,
        modulation,
        normed_one,
        inv_one,
        hidden_one,
        query_heads,
        key_heads,
        value_heads,
        log_total,
        attended,
        attn_out,
        normed_two,
        inv_two,
        hidden_two,
        fc1_pre,
        tanh_inner,
        fc1_act,
        mlp_out,
    ) = saved
    count, seq_len, width = attended.shape
    head_count = width // HEAD
    mods = [piece[:, None, :] for piece in jnp.split(modulation, 6, axis=1)]
    shift_one, scale_one, gate_one, shift_two, scale_two, gate_two = mods
    grad_gate_two = jnp.sum(cotangent * mlp_out, axis=1)
    grad_mlp = cotangent * gate_two
    grad_mlp_low = flat_rows(grad_mlp.astype(jnp.bfloat16))
    grad_fc2_bias = jnp.sum(flat_rows(grad_mlp), axis=0)
    grad_fc2 = matmul(flat_rows(fc1_act).T, arrange(grad_mlp_low))
    grad_act = matmul(grad_mlp_low, fc2_weight.T).reshape(fc1_pre.shape)
    slope = 0.5 * (1.0 + tanh_inner) + 0.5 * fc1_pre * (
        1.0 - tanh_inner * tanh_inner
    ) * gelu_scale * (1.0 + 3.0 * gelu_cubic * fc1_pre * fc1_pre)
    grad_pre = grad_act * slope
    grad_pre_low = flat_rows(grad_pre.astype(jnp.bfloat16))
    grad_fc1_bias = jnp.sum(flat_rows(grad_pre), axis=0)
    grad_fc1 = matmul(flat_rows(hidden_two).T, arrange(grad_pre_low))
    grad_hidden_two = matmul(grad_pre_low, fc1_weight.T).reshape(count, seq_len, width)
    grad_shift_two = jnp.sum(grad_hidden_two, axis=1)
    grad_scale_two = jnp.sum(grad_hidden_two * normed_two, axis=1)
    grad_mid = cotangent + norm_back(grad_hidden_two * (1.0 + scale_two), normed_two, inv_two)
    grad_gate_one = jnp.sum(grad_mid * attn_out, axis=1)
    grad_attn = grad_mid * gate_one
    grad_attn_low = flat_rows(grad_attn.astype(jnp.bfloat16))
    grad_proj_bias = jnp.sum(flat_rows(grad_attn), axis=0)
    grad_proj = matmul(flat_rows(attended).T, arrange(grad_attn_low))
    head_shape = (count, seq_len, head_count, HEAD)
    grad_attended = matmul(grad_attn_low, proj_weight.T).astype(jnp.bfloat16).reshape(head_shape)
    scores = head_product("lqhd,lkhd->lhqk", query_heads, key_heads) * HEAD ** (-0.5)
    prob_full = jnp.exp(scores - log_total)
    prob_low = prob_full.astype(jnp.bfloat16)
    grad_value = head_product("lhqk,lqhd->lkhd", prob_low, grad_attended).reshape(
        count * seq_len, width
    )
    grad_prob = head_product("lqhd,lkhd->lhqk", grad_attended, value_heads)
    row_delta = jnp.sum(prob_full * grad_prob, axis=-1, keepdims=True)
    grad_scores = (prob_full * (grad_prob - row_delta) * HEAD ** (-0.5)).astype(jnp.bfloat16)
    grad_query = head_product("lhqk,lkhd->lqhd", grad_scores, key_heads).reshape(
        count * seq_len, width
    )
    grad_key = head_product("lhqk,lqhd->lkhd", grad_scores, query_heads).reshape(
        count * seq_len, width
    )
    grad_query_bias = jnp.sum(grad_query, axis=0)
    grad_value_bias = jnp.sum(grad_value, axis=0)
    grad_qkv_low = jnp.concatenate([grad_query, grad_key, grad_value], axis=1).astype(jnp.bfloat16)
    grad_qkv = matmul(flat_rows(hidden_one).T, arrange(grad_qkv_low))
    grad_hidden_one = matmul(grad_qkv_low, qkv_weight.T).reshape(count, seq_len, width)
    grad_shift_one = jnp.sum(grad_hidden_one, axis=1)
    grad_scale_one = jnp.sum(grad_hidden_one * normed_one, axis=1)
    grad_latent = grad_mid + norm_back(grad_hidden_one * (1.0 + scale_one), normed_one, inv_one)
    grad_mod = jnp.concatenate(
        [
            grad_shift_one,
            grad_scale_one,
            grad_gate_one,
            grad_shift_two,
            grad_scale_two,
            grad_gate_two,
        ],
        axis=1,
    )
    grad_mod_low = grad_mod.astype(jnp.bfloat16)
    grad_ada = matmul(cond_act.T, arrange(grad_mod_low))
    grad_cond_row = matmul(grad_mod_low, ada_weight.T)
    grad_cond = grad_cond_row * sigmoid_c * (1.0 + conds * (1.0 - sigmoid_c))
    grads = (
        grad_ada,
        arrange(jnp.sum(grad_mod, axis=0)),
        grad_qkv,
        arrange(grad_query_bias),
        arrange(grad_value_bias),
        grad_proj,
        arrange(grad_proj_bias),
        grad_fc1,
        arrange(grad_fc1_bias),
        grad_fc2,
        arrange(grad_fc2_bias),
    )
    return (grad_latent, grad_cond, grads)


def keep_order(values):
    return values


def local(
    latents_in,
    conditioning,
    cotangent,
    ada_weight,
    ada_bias,
    qkv_weight,
    query_bias,
    value_bias,
    proj_weight,
    proj_bias,
    fc1_weight,
    fc1_bias,
    fc2_weight,
    fc2_bias,
):
    weights_fwd = (
        lax.all_gather(ada_weight, "shard", axis=1, tiled=True),
        lax.all_gather(ada_bias, "shard", axis=0, tiled=True),
        lax.all_gather(qkv_weight, "shard", axis=1, tiled=True),
        lax.all_gather(query_bias, "shard", axis=0, tiled=True),
        lax.all_gather(value_bias, "shard", axis=0, tiled=True),
        lax.all_gather(proj_weight, "shard", axis=1, tiled=True),
        lax.all_gather(proj_bias, "shard", axis=0, tiled=True),
        lax.all_gather(fc1_weight, "shard", axis=1, tiled=True),
        lax.all_gather(fc1_bias, "shard", axis=0, tiled=True),
        lax.all_gather(fc2_weight, "shard", axis=1, tiled=True),
        lax.all_gather(fc2_bias, "shard", axis=0, tiled=True),
    )
    block_out, saved_all = forward_all(latents_in, conditioning, weights_fwd)
    weights_bwd = (
        lax.all_gather(ada_weight, "shard", axis=1, tiled=True),
        lax.all_gather(ada_bias, "shard", axis=0, tiled=True),
        lax.all_gather(qkv_weight, "shard", axis=1, tiled=True),
        lax.all_gather(query_bias, "shard", axis=0, tiled=True),
        lax.all_gather(value_bias, "shard", axis=0, tiled=True),
        lax.all_gather(proj_weight, "shard", axis=1, tiled=True),
        lax.all_gather(proj_bias, "shard", axis=0, tiled=True),
        lax.all_gather(fc1_weight, "shard", axis=1, tiled=True),
        lax.all_gather(fc1_bias, "shard", axis=0, tiled=True),
        lax.all_gather(fc2_weight, "shard", axis=1, tiled=True),
        lax.all_gather(fc2_bias, "shard", axis=0, tiled=True),
    )
    grad_input, grad_cond, totals = backward_all(cotangent, saved_all, weights_bwd, keep_order)
    group_sums = (
        lax.psum_scatter(totals[0], "shard", scatter_dimension=1, tiled=True),
        lax.psum_scatter(totals[1], "shard", scatter_dimension=0, tiled=True),
        lax.psum_scatter(totals[2], "shard", scatter_dimension=1, tiled=True),
        lax.psum_scatter(totals[3], "shard", scatter_dimension=0, tiled=True),
        lax.psum_scatter(totals[4], "shard", scatter_dimension=0, tiled=True),
        lax.psum_scatter(totals[5], "shard", scatter_dimension=1, tiled=True),
        lax.psum_scatter(totals[6], "shard", scatter_dimension=0, tiled=True),
        lax.psum_scatter(totals[7], "shard", scatter_dimension=1, tiled=True),
        lax.psum_scatter(totals[8], "shard", scatter_dimension=0, tiled=True),
        lax.psum_scatter(totals[9], "shard", scatter_dimension=1, tiled=True),
        lax.psum_scatter(totals[10], "shard", scatter_dimension=0, tiled=True),
    )
    finals = lax.psum(
        (
            group_sums[0],
            group_sums[1],
            group_sums[2],
            group_sums[3],
            group_sums[4],
            group_sums[5],
            group_sums[6],
            group_sums[7],
            group_sums[8],
            group_sums[9],
            group_sums[10],
        ),
        "rep",
    )
    return (
        block_out,
        grad_input,
        grad_cond,
        finals[0],
        finals[1],
        finals[2],
        finals[3],
        finals[4],
        finals[5],
        finals[6],
        finals[7],
        finals[8],
        finals[9],
        finals[10],
    )


def solution(mesh):
    placed = (
        P(("rep", "shard"), None, None),
        P(("rep", "shard"), None),
        P(("rep", "shard"), None, None),
        P(None, "shard"),
        P("shard"),
        P(None, "shard"),
        P("shard"),
        P("shard"),
        P(None, "shard"),
        P("shard"),
        P(None, "shard"),
        P("shard"),
        P(None, "shard"),
        P("shard"),
    )
    return jax.shard_map(
        local,
        mesh=mesh,
        in_specs=placed,
        out_specs=(
            P(("rep", "shard"), None, None),
            P(("rep", "shard"), None, None),
            P(("rep", "shard"), None),
            P(None, "shard"),
            P("shard"),
            P(None, "shard"),
            P("shard"),
            P("shard"),
            P(None, "shard"),
            P("shard"),
            P(None, "shard"),
            P("shard"),
            P(None, "shard"),
            P("shard"),
        ),
        check_vma=False,
    )
```

profile of v0, /device:TPU:0, one launch (start us, length us, event | category | flops | bytes accessed | tf_op | source)
XLA Modules:
  0.0 869.6 jit_solution(10159185323933018458)
XLA Ops:
  10.6 1.3 fusion.81
  17.5 32.6 %all-reduce.14 = (bf16[4608]{0:T(1024)(128)(2,1)S(1)}, bf16[768]{0:T(1024)(128)(2,1)S(1)}, bf16[768]{0:T(1024)(128)(2,1)S(1)}, bf16[768]{0:T(1024)(128)(2,1)S(1)}, bf16[768]{0:T(1024)(128)(2,1)S(1)}) all-reduce(bf16[4608]{0:T(1024)(128)(2,1)S(1)} %dynamic-update-slice, ...), channel_id=1, replica_groups=mesh['rep'=4,'shard'=8] {'shard'}, use_global_device_ids=true, to_apply=%add | all-reduce | flops 7680 | bytes 30720
  51.3 13.4 %all-gather = bf16[8,1,384]{2,1,0:T(2,128)(2,1)S(1)} all-gather(bf16[1,1,384]{2,1,0:T(2,128)(2,1)S(1)} %reshape.412), channel_id=1, replica_groups=mesh['rep'=4,'shard'=8] {'shard'}, dimensions={0}, use_global_device_ids=true | all-gather | bytes 6912 | tf_op jit(solution)/shard_map/all_gather | solution.py:272
  66.3 17.9 %all-gather.7.cloned.1.call-done = bf16[768,4608]{0,1:T(8,128)(2,1)} async-done(((bf16[768,576]{0,1:T(8,128)(2,1)}), bf16[768,4608]{0,1:T(8,128)(2,1)}) %all-gather.7.cloned.1.call-update) | async-done | bytes 7077904 | tf_op jit(solution)/shard_map/all_gather | solution.py:264
  84.2 5.0 convolution_reduce_fusion
  89.8 36.1 %all-gather.9.cloned.1.call-done = bf16[768,2304]{0,1:T(8,128)(2,1)} async-done(((bf16[768,288]{0,1:T(8,128)(2,1)}), bf16[768,2304]{0,1:T(8,128)(2,1)}) %all-gather.9.cloned.1.call-update) | async-done | bytes 3538960 | tf_op jit(solution)/shard_map/all_gather | solution.py:266
  125.9 3.2 fusion.73
  129.2 0.9 copy.48
  130.1 0.9 copy.49
  131.2 1.8 multiply_reduce_fusion.1
  134.9 14.3 %all-gather.11.cloned.1.call-done = bf16[768,768]{0,1:T(8,128)(2,1)} async-done(((bf16[768,96]{0,1:T(8,128)(2,1)}), bf16[768,768]{0,1:T(8,128)(2,1)}) %all-gather.11.cloned.1.call-update) | async-done | bytes 1179664 | tf_op jit(solution)/shard_map/all_gather | solution.py:269
  149.2 2.9 fusion.78
  152.1 0.9 copy-done.5
  153.8 48.0 %all-gather.13.cloned.1.call-done = bf16[768,3072]{1,0:T(8,128)(2,1)} async-done(((bf16[768,384]{1,0:T(8,128)(2,1)}), bf16[768,3072]{1,0:T(8,128)(2,1)}) %all-gather.13.cloned.1.call-update) | async-done | bytes 4718608 | tf_op jit(solution)/shard_map/all_gather | solution.py:271
  201.7 5.8 convolution_add_fusion
  207.5 45.6 %all-gather.15.cloned.1.call-done = bf16[3072,768]{0,1:T(8,128)(2,1)} async-done(((bf16[3072,96]{0,1:T(8,128)(2,1)}), bf16[3072,768]{0,1:T(8,128)(2,1)}) %all-gather.15.cloned.1.call-update) | async-done | bytes 4718608 | tf_op jit(solution)/shard_map/all_gather | solution.py:273
  253.1 7.2 fusion.84
  260.4 2.2 fusion.28
  263.4 1.3 copy-done.55
  264.7 4.0 multiply_reduce_fusion.5
  268.7 0.9 copy-done.3
  269.6 1.9 fusion.49
  271.6 2.8 convolution_convert_fusion
  274.4 1.9 copy.52
  276.3 3.3 fusion.85
  279.6 5.2 fusion.21
  284.8 5.8 fusion.80
  290.7 2.2 fusion.79
  293.7 4.1 fusion.41
  297.9 1.1 copy-done.7
  299.5 5.1 fusion.37
  304.7 1.8 copy-done.9
  306.5 6.3 fusion.52
  314.3 3.6 fusion.30
  319.4 6.0 broadcast_multiply_fusion
  325.6 60.3 %reduce-scatter.8.cloned.1.call-done = f32[768,288]{0,1:T(8,128)} async-done(((f32[768,2304]{0,1:T(8,128)}), f32[768,288]{0,1:T(8,128)}) %reduce-scatter.8.cloned.1.call-update) | async-done | bytes 884752 | tf_op jit(solution)/shard_map/reduce_scatter | solution.py:294
  385.9 100.2 %reduce-scatter.12.cloned.1.call-done = f32[768,384]{1,0:T(8,128)} async-done(((f32[768,3072]{1,0:T(8,128)}), f32[768,384]{1,0:T(8,128)}) %reduce-scatter.12.cloned.1.call-update) | async-done | bytes 1179664 | tf_op jit(solution)/shard_map/reduce_scatter | solution.py:299
  486.2 100.2 %reduce-scatter.14.cloned.1.call-done = f32[3072,96]{0,1:T(8,128)} async-done(((f32[3072,768]{0,1:T(8,128)}), f32[3072,96]{0,1:T(8,128)}) %reduce-scatter.14.cloned.1.call-update) | async-done | bytes 1179664 | tf_op jit(solution)/shard_map/reduce_scatter | solution.py:301
  586.4 144.6 %reduce-scatter.6.cloned.1.call-done = f32[768,576]{0,1:T(8,128)} async-done(((f32[768,4608]{0,1:T(8,128)}), f32[768,576]{0,1:T(8,128)}) %reduce-scatter.6.cloned.1.call-update) | async-done | bytes 1769488 | tf_op jit(solution)/shard_map/reduce_scatter | solution.py:292
  733.3 26.4 %all-reduce.11 = (f32[4608]{0:T(1024)S(1)}, f32[768]{0:T(1024)S(1)}, f32[768]{0:T(1024)S(1)}, f32[768]{0:T(1024)S(1)}, f32[3072]{0:T(1024)S(1)}, /*index=5*/f32[768]{0:T(1024)S(1)}) all-reduce(f32[4608]{0:T(1024)S(1)} %reduce.38, f32[768]{0:T(1024)S(1)} %reduce_sum.235, ...), channel_id=3, replica_groups=mesh['rep'=4,'shard'=8] {'shard'}, use_global_device_ids=true, to_apply=%region_19.0.clone | all-reduce | flops 10752 | bytes 86016
  760.2 11.3 %all-reduce.12 = (f32[576]{0:T(1024)}, f32[96]{0:T(128)}, f32[96]{0:T(128)}, f32[96]{0:T(128)}, f32[384]{0:T(512)}, /*index=5*/f32[96]{0:T(128)}) all-reduce(f32[576]{0:T(1024)S(1)} %dynamic-slice.6, f32[96]{0:T(128)S(1)} %dynamic-slice.8, f32[96]{0:T(128)S(1)} %dynamic-slice.10, ...), channel_id=1, replica_groups=mesh['rep'=4,'shard'=8] {'rep'}, use_global_device_ids=true, to_apply=%region_20.0 | all-reduce | flops 1344 | bytes 10752 | tf_op jit(solution)/shard_map/psum | solution.py:304
  771.5 1.2 fusion.33
  772.7 4.6 fusion.24
  777.3 79.2 %all-reduce.17.cloned.1.call-done = (f32[768,576]{0,1:T(8,128)}, f32[768,288]{0,1:T(8,128)}, f32[768,96]{0,1:T(8,128)}, f32[768,384]{1,0:T(8,128)}, f32[3072,96]{0,1:T(8,128)}) async-done(((f32[768,576]{0,1:T(8,128)}, f32[768,288]{0,1:T(8,128)}, f32[768,96]{0,1:T(8,128)}, f32[768,384]{1,0:T(8,128)}, f32[3072,96]{0,1:T(8,128)}), (f32[768,576]{0,1:T(8,128)}, f32[768,288]{0,1:T(8,128)}, f32[768,96]{0,1:T(8,128)}, ...) | async-done | bytes 5308432 | tf_op jit(solution)/shard_map/psum | solution.py:304
  856.5 2.9 copy.81
  859.4 0.9 copy.82
  861.0 1.0 copy.84
  862.1 1.0 copy.85
  (202 shorter events, 20.7 us)
Async XLA Ops:
  7.2 58.7 %copy-start = (f32[1,256,768]{2,1,0:T(8,128)S(1)}, f32[1,256,768]{2,1,0:T(8,128)}, u32[]{:S(2)}) copy-start(f32[1,256,768]{2,1,0:T(8,128)} %param.14) | copy-start | bytes 2359300
  7.2 77.0 %copy-start.38 = (f32[1,768]{1,0:T(1,128)S(1)}, f32[1,768]{1,0:T(1,128)}, u32[]{:S(2)}) copy-start(f32[1,768]{1,0:T(1,128)} %param.15) | copy-start | bytes 9220
  7.2 77.0 %all-gather.7.cloned.1.call-start = ((), (), s32[]{:S(2)}) async-start(), calls=%async_computation.5 | async-start | bytes 7962624 | tf_op jit(solution)/shard_map/all_gather | solution.py:264
  7.9 117.9 %all-gather.9.cloned.1.call-start = ((), (), s32[]{:S(2)}) async-start(), calls=%async_computation.6 | async-start | bytes 3981312 | tf_op jit(solution)/shard_map/all_gather | solution.py:266
  8.7 140.5 %all-gather.11.cloned.1.call-start = ((), (), s32[]{:S(2)}) async-start(), calls=%async_computation.7 | async-start | bytes 1327104 | tf_op jit(solution)/shard_map/all_gather | solution.py:269
  9.4 192.3 %all-gather.13.cloned.1.call-start = ((), (), s32[]{:S(2)}) async-start(), calls=%async_computation.8 | async-start | bytes 5308416 | tf_op jit(solution)/shard_map/all_gather | solution.py:271
  10.0 243.1 %all-gather.15.cloned.1.call-start = ((), (), s32[]{:S(2)}) async-start(), calls=%async_computation.9 | async-start | bytes 5308416 | tf_op jit(solution)/shard_map/all_gather | solution.py:273
  10.6 315.0 %reduce-scatter.10.cloned.1.call-start = ((), (), s32[]{:S(2)}) async-start(), calls=%async_computation.12 | async-start | bytes 2654208 | tf_op jit(solution)/shard_map/reduce_scatter | solution.py:297
  66.0 59.8 %copy-start.29 = (f32[256]{0:T(256)}, f32[256]{0:T(256)S(1)}, u32[]{:S(2)}) copy-start(f32[256]{0:T(256)S(1)} %broadcast_multiply_fusion.6) | copy-start | bytes 3076
  66.3 59.6 %copy-start.33 = (f32[256]{0:T(256)}, f32[256]{0:T(256)S(1)}, u32[]{:S(2)}) copy-start(f32[256]{0:T(256)S(1)} %add_rsqrt_fusion.1) | copy-start | bytes 3076
  131.2 3.0 copy-start.10
  253.1 7.2 copy-start.6
  253.1 7.2 copy-start.46
  253.1 7.2 copy-start.49
  253.1 7.2 copy-start.56
  260.4 3.0 copy-start.8
  260.4 3.0 copy-start.21
  260.4 2.9 copy-start.22
  260.4 2.9 copy-start.32
  260.4 2.9 copy-start.40
  260.4 2.9 copy-start.54
  260.4 4.3 copy-start.55
  271.5 4.8 copy-start.11
  271.5 114.4 %reduce-scatter.8.cloned.1.call-start = ((), (), s32[]{:S(2)}) async-start(), calls=%async_computation.11 | async-start | bytes 7962624 | tf_op jit(solution)/shard_map/reduce_scatter | solution.py:294
  284.8 5.9 copy-start.12
  290.7 3.0 copy-start.1
  290.7 3.0 copy-start.23
  290.7 3.0 copy-start.25
  290.7 3.0 copy-start.30
  290.7 3.0 copy-start.34
  297.8 188.3 %reduce-scatter.12.cloned.1.call-start = ((), (), s32[]{:S(2)}) async-start(), calls=%async_computation.13 | async-start | bytes 10616832 | tf_op jit(solution)/shard_map/reduce_scatter | solution.py:299
  304.6 281.8 %reduce-scatter.14.cloned.1.call-start = ((), (), s32[]{:S(2)}) async-start(), calls=%async_computation.14 | async-start | bytes 10616832 | tf_op jit(solution)/shard_map/reduce_scatter | solution.py:301
  312.9 418.2 %reduce-scatter.6.cloned.1.call-start = ((), (), s32[]{:S(2)}) async-start(), calls=%async_computation.10 | async-start | bytes 15925248 | tf_op jit(solution)/shard_map/reduce_scatter | solution.py:292
  314.3 3.8 copy-start.44
  314.3 3.8 copy-start.36
  314.3 3.8 copy-start.42
  314.3 3.8 copy-start.43
  325.5 407.6 %copy-start.51 = (f32[12,64]{1,0:T(8,128)S(1)}, f32[12,64]{1,0:T(8,128)}, u32[]{:S(2)}) copy-start(f32[12,64]{1,0:T(8,128)} %get-tuple-element.65) | copy-start | bytes 9220
  325.5 407.6 %copy-start.37 = (f32[12,64]{1,0:T(8,128)S(1)}, f32[12,64]{1,0:T(8,128)}, u32[]{:S(2)}) copy-start(f32[12,64]{1,0:T(8,128)} %get-tuple-element.63) | copy-start | bytes 9220
  325.5 407.8 %copy-start.48 = (f32[3072]{0:T(1024)S(1)}, f32[3072]{0:T(1024)}, u32[]{:S(2)}) copy-start(f32[3072]{0:T(1024)} %get-tuple-element.76) | copy-start | bytes 36868
  325.5 407.8 %copy-start.52 = (f32[768]{0:T(1024)S(1)}, f32[768]{0:T(1024)}, u32[]{:S(2)}) copy-start(f32[768]{0:T(1024)} %get-tuple-element.18) | copy-start | bytes 9220
  325.5 407.8 %copy-start.53 = (f32[768]{0:T(1024)S(1)}, f32[768]{0:T(1024)}, u32[]{:S(2)}) copy-start(f32[768]{0:T(1024)} %get-tuple-element.61) | copy-start | bytes 9220
  325.5 446.0 %copy-start.4 = (f32[1,256,768]{2,1,0:T(8,128)S(1)}, f32[1,256,768]{2,1,0:T(8,128)}, u32[]{:S(2)}) copy-start(f32[1,256,768]{2,1,0:T(8,128)} %copy-done.3) | copy-start | bytes 2359300
  325.5 530.9 %all-reduce.17.cloned.1.call-start = ((), (), s32[]{:S(2)}) async-start(), calls=%async_computation.15 | async-start | bytes 10616832 | tf_op jit(solution)/shard_map/psum | solution.py:304
  856.5 3.0 copy-start.20
  856.5 3.9 copy-start.27
  856.5 4.6 copy-start.19
  859.4 2.6 copy-start.18
  (20 other events, 27.7 us)
Sparse Core Ops, SparseCore 0:
  9.7 74.4 all-gather.6
  85.8 40.0 all-gather.8
  127.5 21.6 all-gather.10
  150.6 51.0 all-gather.12
  203.2 49.8 all-gather.14
  271.6 35.7 reduce-scatter.9
  309.8 76.0 reduce-scatter.7
  388.2 97.8 reduce-scatter.11
  488.5 97.8 reduce-scatter.13
  588.6 142.4 reduce-scatter.5
  735.3 121.1 all-reduce.16
where the time goes:
time: 870 us
  waiting for transfers between devices  650 us (75%)
  blocking collectives  83.6 us (10%)
  matrix products  77.6 us (9%)
  local copies, waits for them, and re-layouts  27.8 us (3%)
  between operations  17.7 us (2%)
  other arithmetic  12.4 us (1%)
    reduce_scatter x1, waiting for transfers between devices, local(): lax.psum_scatter(totals[0], 'shard', scatter_dimension=1, tiled=True)  145 us
    reduce_scatter x1, waiting for transfers between devices, local(): lax.psum_scatter(totals[9], 'shard', scatter_dimension=1, tiled=True)  100 us
    reduce_scatter x1, waiting for transfers between devices, local(): lax.psum_scatter(totals[7], 'shard', scatter_dimension=1, tiled=True)  100 us
    psum x1, waiting for transfers between devices, local(): lax.psum((group_sums[0], group_sums[1], group_sums[2], group_sums[3], gro...  79.2 us
    reduce_scatter x1, waiting for transfers between devices, local(): lax.psum_scatter(totals[2], 'shard', scatter_dimension=1, tiled=True)  60.3 us
    unnamed x2, blocking collectives  58.9 us
    dot_general x14, matrix products, matmul(): return jnp.dot(left, right, preferred_element_type=jnp.float32)  58.6 us
    all_gather x1, waiting for transfers between devices, local(): lax.all_gather(fc1_weight, 'shard', axis=1, tiled=True)  48 us
  transfers between devices with their start and end apart: 11, of which 10 were waited for; matrix products, arithmetic and copies ran while one was open for 10% of the time, Pallas kernels for 0%

commit v1 on v0

--- a/solution.py
+++ b/solution.py
@@ -8,6 +8,28 @@
 gelu_scale = math.sqrt(2.0 / math.pi)
 gelu_cubic = 0.044715
 norm_eps = 1e-06
+
+
+def laid_out(blocks, dim):
+    blocks = jnp.moveaxis(blocks, 0, dim)
+    shape = blocks.shape
+    return blocks.reshape(*shape[:dim], shape[dim] * shape[dim + 1], *shape[dim + 2 :])
+
+
+def grow_blocks(shard, axis):
+    size = lax.axis_size(axis)
+    blocks = shard[None]
+    for level in range(size.bit_length() - 1):
+        bit = 1 << level
+        other = lax.ppermute(blocks, axis, [(i, i ^ bit) for i in range(size)])
+        both = jnp.stack([blocks, other])
+        upper = lax.axis_index(axis) >> level & 1
+        blocks = jnp.where(upper == 0, both, both[::-1]).reshape(-1, *shard.shape)
+    return blocks
+
+
+def collect(x, axis, dim):
+    return laid_out(grow_blocks(x, axis), dim)
 
 
 def layer_norm(values):
@@ -268,7 +290,7 @@
         lax.all_gather(value_bias, "shard", axis=0, tiled=True),
         lax.all_gather(proj_weight, "shard", axis=1, tiled=True),
         lax.all_gather(proj_bias, "shard", axis=0, tiled=True),
-        lax.all_gather(fc1_weight, "shard", axis=1, tiled=True),
+        collect(fc1_weight, "shard", 1),
         lax.all_gather(fc1_bias, "shard", axis=0, tiled=True),
         lax.all_gather(fc2_weight, "shard", axis=1, tiled=True),
         lax.all_gather(fc2_bias, "shard", axis=0, tiled=True),

time: 870 us -> 958 us (1.10)
  blocking collectives: 83.6 us -> 203 us
  waiting for transfers between devices: 650 us -> 597 us
    unnamed x2, blocking collectives: 58.9 us -> 178 us
    ppermute x0 -> x3, waiting for transfers between devices: none -> 77 us  [grow_blocks(): other = lax.ppermute(blocks, axis, [(i, i ^ bit) for i in range(size)])]
    all_gather x1, waiting for transfers between devices: 45.6 us -> 0.01 us  [local(): lax.all_gather(fc2_weight, 'shard', axis=1, tiled=True)]
    all_gather x1, waiting for transfers between devices: 36.1 us -> 0.01 us  [local(): lax.all_gather(qkv_weight, 'shard', axis=1, tiled=True)]
    all_gather x1, waiting for transfers between devices: 17.9 us -> 0.01 us  [local(): lax.all_gather(ada_weight, 'shard', axis=1, tiled=True)]
    all_gather x1, waiting for transfers between devices: 48 us -> 32.8 us  [local(): lax.all_gather(fc1_weight, 'shard', axis=1, tiled=True)]
    all_gather x1, waiting for transfers between devices: 14.3 us -> 0.02 us  [local(): lax.all_gather(proj_weight, 'shard', axis=1, tiled=True)]
    unnamed x147 -> x159, local copies, waits for them, and re-layouts: 23.5 us -> 17.5 us
  transfers between devices with their start and end apart: 11 -> 14, of which waited for: 10 -> 8; matrix products, arithmetic and copies ran while one was open for 10% -> 11% of each run, Pallas kernels for 0% -> 0%
where the time goes in v1:
time: 958 us; the launch traced here: 957 us
  waiting for transfers between devices  597 us (62%)
  blocking collectives  203 us (21%)
  matrix products  84.1 us (9%)
  local copies, waits for them, and re-layouts  27.1 us (3%)
  other arithmetic  20.2 us (2%)
  between operations  17.8 us (2%)
    unnamed x2, blocking collectives  178 us
    reduce_scatter x1, waiting for transfers between devices, local(): lax.psum_scatter(totals[0], 'shard', scatter_dimension=1, tiled=True)  145 us
    reduce_scatter x1, waiting for transfers between devices, local(): lax.psum_scatter(totals[9], 'shard', scatter_dimension=1, tiled=True)  100 us
    reduce_scatter x1, waiting for transfers between devices, local(): lax.psum_scatter(totals[7], 'shard', scatter_dimension=1, tiled=True)  100 us
    psum x1, waiting for transfers between devices, local(): lax.psum((group_sums[0], group_sums[1], group_sums[2], group_sums[3], gro...  79.2 us
    ppermute x3, waiting for transfers between devices, grow_blocks(): other = lax.ppermute(blocks, axis, [(i, i ^ bit) for i in range(size)])  77 us
    dot_general x14, matrix products, matmul(): return jnp.dot(left, right, preferred_element_type=jnp.float32)  65.1 us
    reduce_scatter x1, waiting for transfers between devices, local(): lax.psum_scatter(totals[2], 'shard', scatter_dimension=1, tiled=True)  60.3 us
  transfers between devices with their start and end apart: 14, of which 8 were waited for; matrix products, arithmetic and copies ran while one was open for 11% of the time, Pallas kernels for 0%

profile of v1, /device:TPU:0, one launch (start us, length us, event | category | flops | bytes accessed | tf_op | source)
XLA Modules:
  0.0 957.0 jit_solution(5799851253252892337)
XLA Ops:
  10.6 1.8 collective-permute-done
  12.4 1.2 pad_maximum_fusion.2
  13.9 3.0 collective-permute-start.1
  17.0 75.1 %collective-permute-done.1 = bf16[2,768,384]{2,1,0:T(8,128)(2,1)S(1)} collective-permute-done((bf16[2,768,384]{2,1,0:T(8,128)(2,1)S(1)}, bf16[2,768,384]{2,1,0:T(8,128)(2,1)S(1)}, u32[]{:S(2)}, u32[]{:S(2)}) %collective-permute-start.1) | collective-permute-done | bytes 1179680 | tf_op jit(solution)/shard_map/ppermute | solution.py:24
  93.0 2.6 copy.54
  95.6 3.5 collective-permute-start.2
  102.2 151.7 %all-reduce.14 = (bf16[4608]{0:T(1024)(128)(2,1)S(1)}, bf16[768]{0:T(1024)(128)(2,1)S(1)}, bf16[768]{0:T(1024)(128)(2,1)S(1)}, bf16[768]{0:T(1024)(128)(2,1)S(1)}, bf16[768]{0:T(1024)(128)(2,1)S(1)}) all-reduce(bf16[4608]{0:T(1024)(128)(2,1)S(1)} %dynamic-update-slice, ...), channel_id=1, replica_groups=mesh['rep'=4,'shard'=8] {'shard'}, use_global_device_ids=true, to_apply=%add | all-reduce | flops 7680 | bytes 30720
  254.6 13.4 %all-gather = bf16[8,1,384]{2,1,0:T(2,128)(2,1)S(1)} all-gather(bf16[1,1,384]{2,1,0:T(2,128)(2,1)S(1)} %reshape.428), channel_id=1, replica_groups=mesh['rep'=4,'shard'=8] {'shard'}, dimensions={0}, use_global_device_ids=true | all-gather | bytes 6912 | tf_op jit(solution)/shard_map/all_gather | solution.py:294
  269.6 2.6 copy.55
  272.2 2.9 pad_maximum_fusion
  275.1 3.1 reverse_select_fusion
  278.3 5.0 convolution_reduce_fusion
  284.0 3.2 fusion.75
  287.4 0.9 copy.50
  288.3 0.9 copy.51
  289.4 1.8 multiply_reduce_fusion.1
  293.1 2.9 fusion.80
  296.9 5.7 convolution_add_fusion
  302.6 8.2 fusion.86
  310.8 32.8 %all-gather.15.cloned.1.call-done = bf16[768,3072]{1,0:T(8,128)(2,1)} async-done(((bf16[768,384]{1,0:T(8,128)(2,1)}), bf16[768,3072]{1,0:T(8,128)(2,1)}) %all-gather.15.cloned.1.call-update) | async-done | bytes 4718608 | tf_op jit(solution)/shard_map/all_gather | solution.py:307
  343.7 5.3 fusion.30
  349.7 6.4 multiply_reduce_fusion.5
  357.0 1.9 fusion.51
  359.0 2.8 convolution_convert_fusion
  361.8 1.9 copy.56
  363.7 3.3 fusion.87
  367.0 5.2 fusion.21
  372.2 5.9 fusion.82
  378.1 2.2 fusion.81
  381.0 4.1 fusion.43
  385.2 1.1 copy-done.7
  386.8 5.1 fusion.39
  392.3 1.6 copy-done.9
  393.9 6.3 fusion.54
  401.7 3.5 fusion.32
  406.8 6.0 broadcast_multiply_fusion
  413.0 60.3 %reduce-scatter.8.cloned.1.call-done = f32[768,288]{0,1:T(8,128)} async-done(((f32[768,2304]{0,1:T(8,128)}), f32[768,288]{0,1:T(8,128)}) %reduce-scatter.8.cloned.1.call-update) | async-done | bytes 884752 | tf_op jit(solution)/shard_map/reduce_scatter | solution.py:316
  473.3 100.2 %reduce-scatter.12.cloned.1.call-done = f32[768,384]{1,0:T(8,128)} async-done(((f32[768,3072]{1,0:T(8,128)}), f32[768,384]{1,0:T(8,128)}) %reduce-scatter.12.cloned.1.call-update) | async-done | bytes 1179664 | tf_op jit(solution)/shard_map/reduce_scatter | solution.py:321
  573.5 100.2 %reduce-scatter.14.cloned.1.call-done = f32[3072,96]{0,1:T(8,128)} async-done(((f32[3072,768]{0,1:T(8,128)}), f32[3072,96]{0,1:T(8,128)}) %reduce-scatter.14.cloned.1.call-update) | async-done | bytes 1179664 | tf_op jit(solution)/shard_map/reduce_scatter | solution.py:323
  673.7 144.7 %reduce-scatter.6.cloned.1.call-done = f32[768,576]{0,1:T(8,128)} async-done(((f32[768,4608]{0,1:T(8,128)}), f32[768,576]{0,1:T(8,128)}) %reduce-scatter.6.cloned.1.call-update) | async-done | bytes 1769488 | tf_op jit(solution)/shard_map/reduce_scatter | solution.py:314
  820.7 26.4 %all-reduce.11 = (f32[4608]{0:T(1024)S(1)}, f32[768]{0:T(1024)S(1)}, f32[768]{0:T(1024)S(1)}, f32[768]{0:T(1024)S(1)}, f32[3072]{0:T(1024)S(1)}, /*index=5*/f32[768]{0:T(1024)S(1)}) all-reduce(f32[4608]{0:T(1024)S(1)} %reduce.38, f32[768]{0:T(1024)S(1)} %reduce_sum.235, ...), channel_id=3, replica_groups=mesh['rep'=4,'shard'=8] {'shard'}, use_global_device_ids=true, to_apply=%region_19.20.clone | all-reduce | flops 10752 | bytes 86016
  847.5 11.3 %all-reduce.12 = (f32[576]{0:T(1024)}, f32[96]{0:T(128)}, f32[96]{0:T(128)}, f32[96]{0:T(128)}, f32[384]{0:T(512)}, /*index=5*/f32[96]{0:T(128)}) all-reduce(f32[576]{0:T(1024)S(1)} %dynamic-slice.6, f32[96]{0:T(128)S(1)} %dynamic-slice.8, f32[96]{0:T(128)S(1)} %dynamic-slice.10, ...), channel_id=1, replica_groups=mesh['rep'=4,'shard'=8] {'rep'}, use_global_device_ids=true, to_apply=%region_20.21 | all-reduce | flops 1344 | bytes 10752 | tf_op jit(solution)/shard_map/psum | solution.py:326
  858.8 1.2 fusion.35
  860.0 4.6 fusion.24
  864.6 79.2 %all-reduce.17.cloned.1.call-done = (f32[768,576]{0,1:T(8,128)}, f32[768,288]{0,1:T(8,128)}, f32[768,96]{0,1:T(8,128)}, f32[768,384]{1,0:T(8,128)}, f32[3072,96]{0,1:T(8,128)}) async-done(((f32[768,576]{0,1:T(8,128)}, f32[768,288]{0,1:T(8,128)}, f32[768,96]{0,1:T(8,128)}, f32[768,384]{1,0:T(8,128)}, f32[3072,96]{0,1:T(8,128)}), (f32[768,576]{0,1:T(8,128)}, f32[768,288]{0,1:T(8,128)}, f32[768,96]{0,1:T(8,128)}, ...) | async-done | bytes 5308432 | tf_op jit(solution)/shard_map/psum | solution.py:326
  943.8 2.9 copy.85
  948.4 1.0 copy.88
  949.4 1.0 copy.89
  (228 shorter events, 20.9 us)
Async XLA Ops:
  7.2 271.1 %all-gather.7.cloned.1.call-start = ((), (), s32[]{:S(2)}) async-start(), calls=%async_computation.5 | async-start | bytes 7962624 | tf_op jit(solution)/shard_map/all_gather | solution.py:286
  7.9 276.1 %all-gather.9.cloned.1.call-start = ((), (), s32[]{:S(2)}) async-start(), calls=%async_computation.6 | async-start | bytes 3981312 | tf_op jit(solution)/shard_map/all_gather | solution.py:288
  8.7 284.4 %all-gather.11.cloned.1.call-start = ((), (), s32[]{:S(2)}) async-start(), calls=%async_computation.7 | async-start | bytes 1327104 | tf_op jit(solution)/shard_map/all_gather | solution.py:291
  9.4 293.2 %all-gather.13.cloned.1.call-start = ((), (), s32[]{:S(2)}) async-start(), calls=%async_computation.8 | async-start | bytes 5308416 | tf_op jit(solution)/shard_map/all_gather | solution.py:295
  10.0 333.6 %all-gather.15.cloned.1.call-start = ((), (), s32[]{:S(2)}) async-start(), calls=%async_computation.9 | async-start | bytes 5308416 | tf_op jit(solution)/shard_map/all_gather | solution.py:307
  10.0 2.4 collective-permute-start
  13.9 78.2 %collective-permute-start.1 = (bf16[2,768,384]{2,1,0:T(8,128)(2,1)S(1)}, bf16[2,768,384]{2,1,0:T(8,128)(2,1)S(1)}, u32[]{:S(2)}, u32[]{:S(2)}) collective-permute-start(bf16[2,768,384]{2,1,0:T(8,128)(2,1)S(1)} %get-tuple-element.60), channel_id=1, source_target_pairs={{0,2},{1,3},{2,0},{3,1},{4,6},{5,7},{6,4},{7,5},{8,10},{9,11},{10,... | collective-permute-start | bytes 3538952 | tf_op jit(solution)/shard_map/ppermute | solution.py:24
  16.9 396.0 %reduce-scatter.10.cloned.1.call-start = ((), (), s32[]{:S(2)}) async-start(), calls=%async_computation.12 | async-start | bytes 2654208 | tf_op jit(solution)/shard_map/reduce_scatter | solution.py:319
  92.9 6.2 copy-start.56
  92.9 8.1 copy-start.59
  92.9 8.3 copy-start.60
  93.0 8.6 copy-start.61
  93.0 8.8 copy-start.62
  93.0 9.0 copy-start.57
  93.0 161.6 %copy-start.58 = (bf16[384]{0:T(512)(128)(2,1)S(1)}, bf16[384]{0:T(512)(128)(2,1)}, u32[]{:S(2)}) copy-start(bf16[384]{0:T(512)(128)(2,1)} %param.25) | copy-start | bytes 2308
  93.0 176.2 %copy-start = (f32[1,256,768]{2,1,0:T(8,128)S(1)}, f32[1,256,768]{2,1,0:T(8,128)}, u32[]{:S(2)}) copy-start(f32[1,256,768]{2,1,0:T(8,128)} %param.14) | copy-start | bytes 2359300
  95.6 176.6 %collective-permute-start.2 = (bf16[4,768,384]{1,2,0:T(8,128)(2,1)}, bf16[4,768,384]{1,2,0:T(8,128)(2,1)}, u32[]{:S(2)}, u32[]{:S(2)}) collective-permute-start(bf16[4,768,384]{1,2,0:T(8,128)(2,1)} %copy.54), channel_id=1, source_target_pairs={{0,4},{1,5},{2,6},{3,7},{4,0},{5,1},{6,2},{7,3},{8,12},{9,13},{10,... | collective-permute-start | bytes 7077896 | tf_op jit(solution)/shard_map/ppermute | solution.py:24
  269.3 14.7 %copy-start.28 = (f32[256]{0:T(256)}, f32[256]{0:T(256)S(1)}, u32[]{:S(2)}) copy-start(f32[256]{0:T(256)S(1)} %broadcast_multiply_fusion.6) | copy-start | bytes 3076
  269.6 14.4 %copy-start.32 = (f32[256]{0:T(256)}, f32[256]{0:T(256)S(1)}, u32[]{:S(2)}) copy-start(f32[256]{0:T(256)S(1)} %add_rsqrt_fusion.1) | copy-start | bytes 3076
  293.1 3.8 copy-start.47
  343.6 6.0 copy-start.6
  343.6 6.0 copy-start.8
  343.6 6.0 copy-start.20
  343.6 6.0 copy-start.21
  343.6 6.1 copy-start.31
  343.6 6.1 copy-start.39
  343.6 6.1 copy-start.45
  343.7 6.1 copy-start.50
  343.7 6.1 copy-start.55
  358.9 4.8 copy-start.11
  358.9 114.3 %reduce-scatter.8.cloned.1.call-start = ((), (), s32[]{:S(2)}) async-start(), calls=%async_computation.11 | async-start | bytes 7962624 | tf_op jit(solution)/shard_map/reduce_scatter | solution.py:316
  372.2 5.9 copy-start.12
  385.2 188.3 %reduce-scatter.12.cloned.1.call-start = ((), (), s32[]{:S(2)}) async-start(), calls=%async_computation.13 | async-start | bytes 10616832 | tf_op jit(solution)/shard_map/reduce_scatter | solution.py:321
  392.0 281.7 %reduce-scatter.14.cloned.1.call-start = ((), (), s32[]{:S(2)}) async-start(), calls=%async_computation.14 | async-start | bytes 10616832 | tf_op jit(solution)/shard_map/reduce_scatter | solution.py:323
  400.3 418.1 %reduce-scatter.6.cloned.1.call-start = ((), (), s32[]{:S(2)}) async-start(), calls=%async_computation.10 | async-start | bytes 15925248 | tf_op jit(solution)/shard_map/reduce_scatter | solution.py:314
  401.7 3.8 copy-start.43
  401.7 3.8 copy-start.35
  401.7 3.8 copy-start.41
  401.7 3.8 copy-start.42
  412.8 407.5 %copy-start.52 = (f32[12,64]{1,0:T(8,128)S(1)}, f32[12,64]{1,0:T(8,128)}, u32[]{:S(2)}) copy-start(f32[12,64]{1,0:T(8,128)} %get-tuple-element.67) | copy-start | bytes 9220
  412.8 407.6 %copy-start.36 = (f32[12,64]{1,0:T(8,128)S(1)}, f32[12,64]{1,0:T(8,128)}, u32[]{:S(2)}) copy-start(f32[12,64]{1,0:T(8,128)} %get-tuple-element.65) | copy-start | bytes 9220
  412.9 407.8 %copy-start.48 = (f32[3072]{0:T(1024)S(1)}, f32[3072]{0:T(1024)}, u32[]{:S(2)}) copy-start(f32[3072]{0:T(1024)} %get-tuple-element.78) | copy-start | bytes 36868
  412.9 407.8 %copy-start.53 = (f32[768]{0:T(1024)S(1)}, f32[768]{0:T(1024)}, u32[]{:S(2)}) copy-start(f32[768]{0:T(1024)} %get-tuple-element.18) | copy-start | bytes 9220
  412.9 407.8 %copy-start.54 = (f32[768]{0:T(1024)S(1)}, f32[768]{0:T(1024)}, u32[]{:S(2)}) copy-start(f32[768]{0:T(1024)} %get-tuple-element.63) | copy-start | bytes 9220
  412.9 446.0 %copy-start.4 = (f32[1,256,768]{2,1,0:T(8,128)S(1)}, f32[1,256,768]{2,1,0:T(8,128)}, u32[]{:S(2)}) copy-start(f32[1,256,768]{2,1,0:T(8,128)} %copy-done.3) | copy-start | bytes 2359300
  412.9 530.9 %all-reduce.17.cloned.1.call-start = ((), (), s32[]{:S(2)}) async-start(), calls=%async_computation.15 | async-start | bytes 10616832 | tf_op jit(solution)/shard_map/psum | solution.py:326
  943.8 3.9 copy-start.26
  943.8 4.6 copy-start.18
  (29 other events, 52.4 us)
Sparse Core Ops, SparseCore 0:
  9.6 92.2 all-gather.6
  103.6 93.7 all-gather.8
  199.0 25.9 all-gather.10
  226.5 65.3 all-gather.12
  293.4 50.2 all-gather.14
  359.1 35.6 reduce-scatter.9
  397.1 76.1 reduce-scatter.7
  475.6 97.8 reduce-scatter.11
  575.8 97.8 reduce-scatter.13
  675.9 142.4 reduce-scatter.5
  822.6 121.1 all-reduce.16
